TPU v7x, 32 devices: a whole 2x2x4 slice. The times are simulated.
32 devices in a mesh: tm: 2 (over x), diamond: 2 (over y), tile: 8 (over z, core).
Axes of the slice: x: 2, y: 2, z: 4, core: 2. Of those that a mesh axis runs over, the one named last changes fastest.
Arguments:
- activations: bfloat16 [8, 2, 32, 64, 256], P('tm', 'diamond', 'tile'), may hold values from -6 to 6
- upstream: bfloat16 [8, 2, 32, 64, 256], P('tm', 'diamond', 'tile'), may hold values from -16 to 16
- hex_weight: bfloat16 [7, 64, 64], replicated, may hold values from -0.25 to 0.25
- time_weight: bfloat16 [3, 64, 64], replicated, may hold values from -0.4375 to 0.4375
- left_map: int32 [2, 32], replicated, may hold values from 0 to 31, each once within a row
- right_map: int32 [2, 32], replicated, may hold values from 0 to 31, each once within a row
Outputs:
- grad_input: bfloat16 [8, 2, 32, 64, 256], P('tm', 'diamond', 'tile')
- grad_hex: float32 [7, 64, 64], replicated
- grad_time: float32 [3, 64, 64], replicated
Inputs may be any that keep to these rules, and one draw needn't show every extreme that they name: Each row of left_map holds every number of 0 to 31 once. Each row of right_map holds every number of 0 to 31 once.
All inputs are finite; a program needn't handle non-finite values.
Results may differ from a plain program's by a relative error of at most 0.0035.
Values may be sent and summed in bfloat16 or wider, within the bound.
A program may use at most 64 MiB of HBM per device.

v0:
```python
import jax
import jax.numpy as jnp
from jax import lax
from jax.sharding import PartitionSpec as P

OFFSETS = ((0, 0), (0, 1), (0, -1), (1, 0), (-1, 0), (1, -1), (-1, 1))


def from_behind(block, axis, distance):
    devices = range(lax.axis_size(axis))
    route = [((i - distance) % len(devices), i) for i in devices]
    return lax.ppermute(block, axis, route)


def with_halo(x, sides, width):
    for axis, dim in sides:
        size, length = (lax.axis_size(axis), x.shape[dim])
        up = [(i, (i + 1) % size) for i in range(size - 1)]
        down = [(j, i) for i, j in up]
        last = lax.slice_in_dim(x, length - width, length, axis=dim)
        initial = lax.slice_in_dim(x, 0, width, axis=dim)
        before = lax.ppermute(last, axis, up)
        after = lax.ppermute(initial, axis, down)
        x = jnp.concatenate([before, x, after], axis=dim)
    return x


def passed_along(block, axis, distance):
    devices = range(lax.axis_size(axis))
    route = [(i - distance, i) for i in devices if i - distance in devices]
    return lax.ppermute(block, axis, route)


def silu_slope(hidden):
    sigmoid = jax.nn.sigmoid(hidden)
    return sigmoid * (1.0 + hidden * (1.0 - sigmoid))


def shards(activations, upstream, hex_weight, time_weight, left_map, right_map):
    field = activations[:, 0]
    cotangent = upstream[:, 0]
    frames, tile_rows, channels, columns = field.shape
    chart = lax.axis_index("diamond")
    first_row = lax.axis_index("tile") * tile_rows
    chart_rows = tile_rows * lax.axis_size("tile")
    own_left = lax.dynamic_slice(left_map, (chart, first_row), (1, tile_rows))[0]
    own_right = lax.dynamic_slice(right_map, (chart, first_row), (1, tile_rows))[0]
    strips = (
        lax.all_gather(field[..., 0], "tile", axis=1, tiled=True),
        lax.all_gather(field[..., columns - 1], "tile", axis=1, tiled=True),
    )
    prev_right = from_behind(strips[1], "diamond", 1)
    next_left = from_behind(strips[0], "diamond", -1)
    ghost_left = jnp.take(prev_right, own_left, axis=1)
    ghost_right = jnp.take(next_left, own_right, axis=1)
    widened = jnp.concatenate([ghost_left[..., None], field, ghost_right[..., None]], axis=-1)
    depth = 1
    margin = depth - 1
    span_rows = tile_rows + 2 * margin
    padded = with_halo(widened, (("tile", 1),), depth)
    hidden = jnp.zeros((frames, span_rows, channels, columns), jnp.float32)
    for number, (step_row, step_col) in enumerate(OFFSETS):
        window = padded[
            :, 1 + step_row : 1 + step_row + span_rows, :, 1 + step_col : 1 + step_col + columns
        ]
        hidden = hidden + jnp.einsum(
            "frcx,cd->frdx", window, hex_weight[number], preferred_element_type=jnp.float32
        )
    active = jax.nn.silu(hidden).astype(jnp.bfloat16)
    framed = with_halo(cotangent, (("tm", 0),), 1)
    grad_act = jnp.zeros((frames, span_rows, channels, columns), jnp.float32)
    time_terms = []
    for number in range(3):
        shifted = framed[2 - number : 2 - number + frames]
        grad_act = grad_act + jnp.einsum(
            "frdx,cd->frcx", shifted, time_weight[number], preferred_element_type=jnp.float32
        )
        time_terms.append(
            jnp.einsum("frcx,frdx->cd", active, shifted, preferred_element_type=jnp.float32)
        )
    grad_wide = (grad_act * silu_slope(hidden)).astype(jnp.bfloat16)
    hex_terms = []
    for number, (step_row, step_col) in enumerate(OFFSETS):
        begin = 1 + margin + step_row
        window = padded[:, begin : begin + tile_rows, :, 1 + step_col : 1 + step_col + columns]
        hex_terms.append(
            jnp.einsum("frcx,frdx->cd", window, grad_wide, preferred_element_type=jnp.float32)
        )
    spread = jnp.zeros((frames, tile_rows + 2, channels, columns + 2), jnp.float32)
    for number, (step_row, step_col) in enumerate(OFFSETS):
        spread = spread.at[
            :, 1 + step_row : 1 + step_row + tile_rows, :, 1 + step_col : 1 + step_col + columns
        ].add(
            jnp.einsum(
                "frdx,cd->frcx", grad_wide, hex_weight[number], preferred_element_type=jnp.float32
            )
        )
    from_below = passed_along(spread[:, 0].astype(jnp.bfloat16), "tile", -1).astype(jnp.float32)
    from_above = passed_along(spread[:, tile_rows + 1].astype(jnp.bfloat16), "tile", 1).astype(
        jnp.float32
    )
    owned = spread[:, 1 : tile_rows + 1]
    owned = owned.at[:, 0].add(from_above)
    owned = owned.at[:, tile_rows - 1].add(from_below)
    total = cotangent.astype(jnp.float32) + owned[..., 1 : columns + 1]
    left_grad = owned[..., 0]
    right_grad = owned[..., columns + 1]
    strip_left = (
        jnp.zeros((frames, chart_rows, channels), jnp.float32).at[:, own_left].set(left_grad)
    )
    strip_right = (
        jnp.zeros((frames, chart_rows, channels), jnp.float32).at[:, own_right].set(right_grad)
    )
    moved_left = from_behind(strip_left.astype(jnp.bfloat16), "diamond", -1).astype(
        strip_left.dtype
    )
    moved_right = from_behind(strip_right.astype(jnp.bfloat16), "diamond", 1).astype(
        strip_right.dtype
    )
    into_last, into_first = (
        lax.psum_scatter(
            moved_left.astype(jnp.bfloat16), "tile", scatter_dimension=1, tiled=True
        ).astype(jnp.float32),
        lax.psum_scatter(
            moved_right.astype(jnp.bfloat16), "tile", scatter_dimension=1, tiled=True
        ).astype(jnp.float32),
    )
    total = total.at[..., columns - 1].add(into_last)
    total = total.at[..., 0].add(into_first)
    hex_local = jnp.stack(hex_terms)
    time_local = jnp.stack(time_terms)
    grad_hex, grad_time = lax.psum((hex_local, time_local), ("tm", "diamond", "tile"))
    return (total.astype(jnp.bfloat16)[:, None], grad_hex, grad_time)


def solution(mesh):
    in_specs = (
        P("tm", "diamond", "tile", None, None),
        P("tm", "diamond", "tile", None, None),
        P(),
        P(),
        P(),
        P(),
    )
    out_specs = (P("tm", "diamond", "tile", None, None), P(), P())
    return jax.shard_map(shards, mesh=mesh, in_specs=in_specs, out_specs=out_specs, check_vma=False)
```

profile of v0, /device:TPU:0, one launch (start us, length us, event | category | flops | bytes accessed | tf_op | source)
XLA Modules:
  0.0 317.2 jit_solution(10565177064639616680)
XLA Ops:
  8.4 25.1 %all-gather = bf16[4,32,64,1]{3,2,1,0:T(8,128)(2,1)S(1)} all-gather(bf16[4,4,64,1]{3,2,1,0:T(8,128)(2,1)S(1)} %get-tuple-element.164), channel_id=2, replica_groups=mesh['tm'=2,'diamond'=2,'tile'=8] {'tile'}, dimensions={1}, use_global_device_ids=true | all-gather | bytes 18432 | tf_op jit(solution)/shard_map/all_gather | solution.py:49
  34.6 1.6 collective-permute-start.2
  36.2 22.7 %all-gather.1 = bf16[4,32,64,1]{3,2,1,0:T(8,128)(2,1)S(1)} all-gather(bf16[4,4,64,1]{3,2,1,0:T(8,128)(2,1)S(1)} %get-tuple-element.163), channel_id=3, replica_groups=mesh['tm'=2,'diamond'=2,'tile'=8] {'tile'}, dimensions={1}, use_global_device_ids=true | all-gather | bytes 18432 | tf_op jit(solution)/shard_map/all_gather | solution.py:50
  61.2 4.2 %collective-permute-start.1 = (bf16[1,4,64,256]{3,2,1,0:T(8,128)(2,1)}, bf16[1,4,64,256]{3,2,1,0:T(8,128)(2,1)}, u32[]{:S(2)}, u32[]{:S(2)}) collective-permute-start(bf16[1,4,64,256]{3,2,1,0:T(8,128)(2,1)} %get-tuple-element.162), channel_id=1, source_target_pairs={{0,16},{1,17},{2,18},{3,19},{4,20},{5,21},{6,22},{7,23},{8,24},{9,... | collective-permute-start | bytes 393224 | tf_op jit(solution)/shard_map/ppermute | solution.py:22
  65.4 1.3 collective-permute-start
  69.1 2.7 and_reduce_fusion
  76.3 1.4 collective-permute-start.4
  77.7 3.2 %collective-permute-start.5 = (bf16[4,1,64,258]{3,2,1,0:T(8,128)(2,1)S(1)}, bf16[4,1,64,258]{3,2,1,0:T(8,128)(2,1)S(1)}, u32[]{:S(2)}, u32[]{:S(2)}) collective-permute-start(bf16[4,1,64,258]{3,2,1,0:T(8,128)(2,1)S(1)} %get-tuple-element.160), channel_id=1, source_target_pairs={{0,1},{1,2},{2,3},{3,4},{4,5},{5,6},{6,7},{8,9},{9,10},{10,11},{11... | collective-permute-start | bytes 396296 | tf_op jit(solution)/shard_map/ppermute | solution.py:22
  84.5 1.5 multiply_convert_fusion
  86.0 1.5 fusion.15
  88.7 1.4 fusion.9
  90.5 7.1 %scatter-add.39 = f32[4,6,64,258]{3,2,0,1:T(8,128)S(1)} dynamic-update-slice(f32[4,6,64,258]{3,2,0,1:T(8,128)S(1)} %scatter-add.36, f32[4,4,64,256]{3,2,0,1:T(8,128)} %fusion.9, s32[]{:T(128)} %constant.332.clone.1, s32[]{:T(128)} %constant.338.clone.1, s32[]{:T(128)} %constant.332.clone.1, s32[]{:T(128)} %constant.333.clone.1) | dynamic-update-slice | bytes 2097156 | tf_op jit(solution)/shard_map/scatter-add | solution.py:93
  97.9 1.3 fusion.12
  99.3 7.1 %scatter-add.41 = f32[4,6,64,258]{3,2,0,1:T(8,128)S(1)} dynamic-update-slice(f32[4,6,64,258]{3,2,0,1:T(8,128)S(1)} %fusion.11, f32[4,4,64,256]{3,2,0,1:T(8,128)} %fusion.12, s32[]{:T(128)} %constant.332.clone.1, s32[]{:T(128)} %constant.333.clone.1, s32[]{:T(128)} %constant.332.clone.1, s32[]{:T(128)} %constant.338.clone.1) | dynamic-update-slice | bytes 2097156 | tf_op jit(solution)/shard_map/scatter-add | solution.py:93
  106.3 2.7 add_select_fusion.1
  109.0 7.8 %scatter-add.44 = f32[4,6,64,258]{3,2,0,1:T(8,128)S(1)} dynamic-update-slice(f32[4,6,64,258]{3,2,0,1:T(8,128)S(1)} %scatter-add.41, f32[4,4,64,256]{3,2,0,1:T(8,128)} %add_select_fusion.1, s32[]{:T(128)} %constant.332.clone.1, s32[]{:T(128)S(1)} %bitcast.366, s32[]{:T(128)} %constant.332.clone.1, s32[]{:T(128)} %bitcast.61) | dynamic-update-slice | bytes 2097156 | tf_op jit(solution)/shard_map/scatter-add | solution.py:93
  117.1 3.2 add_select_fusion
  120.3 8.4 %scatter-add.46 = f32[4,6,64,258]{3,2,0,1:T(8,128)S(1)} dynamic-update-slice(f32[4,6,64,258]{3,2,0,1:T(8,128)S(1)} %fusion.14, f32[4,4,64,256]{3,2,0,1:T(8,128)} %add_select_fusion, s32[]{:T(128)} %constant.332.clone.1, s32[]{:T(128)} %bitcast.66, s32[]{:T(128)} %constant.332.clone.1, s32[]{:T(128)} %bitcast.67) | dynamic-update-slice | bytes 2097156 | tf_op jit(solution)/shard_map/scatter-add | solution.py:93
  129.9 1.3 slice.528
  137.2 1.4 convolution_bitcast_fusion.18
  138.6 1.8 slice_bitcast_fusion.1
  140.4 4.4 %collective-permute-start.6 = (bf16[4,64,258]{2,1,0:T(8,128)(2,1)}, bf16[4,64,258]{2,1,0:T(8,128)(2,1)}, u32[]{:S(2)}, u32[]{:S(2)}) collective-permute-start(bf16[4,64,258]{2,1,0:T(8,128)(2,1)} %get-tuple-element.156), channel_id=1, source_target_pairs={{0,1},{1,2},{2,3},{3,4},{4,5},{5,6},{6,7},{8,9},{9,10},{10,11},{11... | collective-permute-start | bytes 396296 | tf_op jit(solution)/shard_map/ppermute | solution.py:31
  146.1 1.3 convolution_bitcast_fusion.17
  148.7 45.7 %psum.15 = f32[3,64,64]{2,1,0:T(8,128)} all-reduce(f32[3,64,64]{2,1,0:T(8,128)S(1)} %pad_maximum_fusion.16), channel_id=1, replica_groups=mesh['tm'=2,'diamond'=2,'tile'=8] {'tm','diamond','tile'}, use_global_device_ids=true, to_apply=%region_7.9 | all-reduce | flops 12288 | bytes 98304 | tf_op jit(solution)/shard_map/psum | solution.py:132
  194.3 71.3 %all-reduce.6.cloned.1.call-done = f32[7,64,64]{1,2,0:T(8,128)} async-done(((f32[7,64,64]{1,2,0:T(8,128)}), f32[7,64,64]{1,2,0:T(8,128)}) %all-reduce.6.cloned.1.call-update) | async-done | bytes 114704 | tf_op jit(solution)/shard_map/psum | solution.py:132
  265.6 1.8 copy.133
  267.4 1.7 fusion.33
  269.1 1.5 copy.119
  273.0 1.5 collective-permute-start.8
  277.2 1.9 collective-permute-done.9
  279.1 26.9 %all-reduce.3 = (bf16[4,32,64]{2,0,1:T(4,128)(2,1)S(1)}, bf16[4,32,64]{2,0,1:T(4,128)(2,1)S(1)}) all-reduce(bf16[4,32,64]{2,0,1:T(4,128)(2,1)S(1)} %collective-permute-done.8, bf16[4,32,64]{2,0,1:T(4,128)(2,1)S(1)} %collective-permute-done.9), channel_id=4, replica_groups=mesh['tm'=2,'diamond'=2,'tile'=8] {'tile'}, use_global_device_ids=true, to_apply=%region_3.5.clone | all-reduce | flops 16384 | bytes 65536
  306.8 1.9 scatter-add.51
  (116 shorter events, 33.3 us)
Async XLA Ops:
  7.2 258.5 %all-reduce.6.cloned.1.call-start = ((), (), s32[]{:S(2)}) async-start(), calls=%async_computation | async-start | bytes 458752 | tf_op jit(solution)/shard_map/psum | solution.py:132
  34.6 38.7 %collective-permute-start.2 = (bf16[4,32,64]{2,0,1:T(4,128)(2,1)S(1)}, bf16[4,32,64]{2,0,1:T(4,128)(2,1)S(1)}, u32[]{:S(2)}, u32[]{:S(2)}) collective-permute-start(bf16[4,32,64]{2,0,1:T(4,128)(2,1)S(1)} %bitcast.359), channel_id=1, source_target_pairs={{8,0},{0,8},{9,1},{1,9},{10,2},{2,10},{11,3},{3,11},{12,4},{4,12},... | collective-permute-start | bytes 49160 | tf_op jit(solution)/shard_map/ppermute | solution.py:12
  36.1 24.3 %copy-start.1 = (bf16[4,1,4,64,256]{4,3,2,1,0:T(8,128)(2,1)S(1)}, bf16[4,1,4,64,256]{4,3,2,1,0:T(8,128)(2,1)}, u32[]{:S(2)}) copy-start(bf16[4,1,4,64,256]{4,3,2,1,0:T(8,128)(2,1)} %param.31) | copy-start | bytes 1572868
  36.1 30.6 %copy-start.14 = (s32[2,32]{1,0:T(2,128)S(1)}, s32[2,32]{1,0:T(2,128)}, u32[]{:S(2)}) copy-start(s32[2,32]{1,0:T(2,128)} %param.35) | copy-start | bytes 772
  36.2 30.6 %copy-start.15 = (s32[2,32]{1,0:T(2,128)S(1)}, s32[2,32]{1,0:T(2,128)}, u32[]{:S(2)}) copy-start(s32[2,32]{1,0:T(2,128)} %param.34) | copy-start | bytes 772
  58.9 10.3 %copy-start.16 = (s32[4]{0:T(128)S(1)}, s32[4]{0:T(128)}, u32[]{:S(2)}) copy-start(s32[4]{0:T(128)} %constant.340.clone.1) | copy-start | bytes 52
  58.9 13.0 %copy-start.17 = (u32[32]{0:T(128)S(1)}, u32[32]{0:T(128)}, u32[]{:S(2)}) copy-start(u32[32]{0:T(128)} %constant.350) | copy-start | bytes 388
  58.9 16.2 %copy-start = (bf16[4,1,4,64,256]{4,3,2,1,0:T(8,128)(2,1)S(1)}, bf16[4,1,4,64,256]{4,3,2,1,0:T(8,128)(2,1)}, u32[]{:S(2)}) copy-start(bf16[4,1,4,64,256]{4,3,2,1,0:T(8,128)(2,1)} %param.30) | copy-start | bytes 1572868
  59.9 14.3 %collective-permute-start.3 = (bf16[4,32,64]{2,0,1:T(4,128)(2,1)S(1)}, bf16[4,32,64]{2,0,1:T(4,128)(2,1)S(1)}, u32[]{:S(2)}, u32[]{:S(2)}) collective-permute-start(bf16[4,32,64]{2,0,1:T(4,128)(2,1)S(1)} %bitcast.358), channel_id=1, source_target_pairs={{8,0},{0,8},{9,1},{1,9},{10,2},{2,10},{11,3},{3,11},{12,4},{4,12},... | collective-permute-start | bytes 49160 | tf_op jit(solution)/shard_map/ppermute | solution.py:12
  61.2 14.2 %copy-start.12 = (bf16[7,64,64]{2,1,0:T(8,128)(2,1)S(1)}, bf16[7,64,64]{2,1,0:T(8,128)(2,1)}, u32[]{:S(2)}) copy-start(bf16[7,64,64]{2,1,0:T(8,128)(2,1)} %param.32) | copy-start | bytes 172036
  61.2 20.0 %collective-permute-start.1 = (bf16[1,4,64,256]{3,2,1,0:T(8,128)(2,1)}, bf16[1,4,64,256]{3,2,1,0:T(8,128)(2,1)}, u32[]{:S(2)}, u32[]{:S(2)}) collective-permute-start(bf16[1,4,64,256]{3,2,1,0:T(8,128)(2,1)} %get-tuple-element.162), channel_id=1, source_target_pairs={{0,16},{1,17},{2,18},{3,19},{4,20},{5,21},{6,22},{7,23},{8,24},{9,... | collective-permute-start | bytes 393224 | tf_op jit(solution)/shard_map/ppermute | solution.py:22
  65.4 20.6 %collective-permute-start = (bf16[1,4,64,256]{3,2,1,0:T(8,128)(2,1)}, bf16[1,4,64,256]{3,2,1,0:T(8,128)(2,1)}, u32[]{:S(2)}, u32[]{:S(2)}) collective-permute-start(bf16[1,4,64,256]{3,2,1,0:T(8,128)(2,1)} %get-tuple-element.161), channel_id=1, source_target_pairs={{16,0},{17,1},{18,2},{19,3},{20,4},{21,5},{22,6},{23,7},{24,8},{25... | collective-permute-start | bytes 393224 | tf_op jit(solution)/shard_map/ppermute | solution.py:23
  74.2 8.3 %copy-start.7 = (bf16[4,4,64,1]{3,2,1,0:T(8,128)(2,1)}, bf16[4,4,64,1]{3,2,1,0:T(8,128)(2,1)S(1)}, u32[]{:S(2)}) copy-start(bf16[4,4,64,1]{3,2,1,0:T(8,128)(2,1)S(1)} %copy.92) | copy-start | bytes 6148
  75.1 7.4 %copy-start.9 = (bf16[4,4,64,1]{3,2,1,0:T(8,128)(2,1)}, bf16[4,4,64,1]{3,2,1,0:T(8,128)(2,1)S(1)}, u32[]{:S(2)}) copy-start(bf16[4,4,64,1]{3,2,1,0:T(8,128)(2,1)S(1)} %copy.96) | copy-start | bytes 6148
  76.2 5.0 %copy-start.13 = (bf16[3,64,64]{2,1,0:T(8,128)(2,1)S(1)}, bf16[3,64,64]{2,1,0:T(8,128)(2,1)}, u32[]{:S(2)}) copy-start(bf16[3,64,64]{2,1,0:T(8,128)(2,1)} %param.33) | copy-start | bytes 73732
  76.3 6.2 %collective-permute-start.4 = (bf16[4,1,64,258]{3,2,1,0:T(8,128)(2,1)S(1)}, bf16[4,1,64,258]{3,2,1,0:T(8,128)(2,1)S(1)}, u32[]{:S(2)}, u32[]{:S(2)}) collective-permute-start(bf16[4,1,64,258]{3,2,1,0:T(8,128)(2,1)S(1)} %get-tuple-element.159), channel_id=1, source_target_pairs={{1,0},{2,1},{3,2},{4,3},{5,4},{6,5},{7,6},{9,8},{10,9},{11,10},{12... | collective-permute-start | bytes 396296 | tf_op jit(solution)/shard_map/ppermute | solution.py:23
  77.7 4.8 %collective-permute-start.5 = (bf16[4,1,64,258]{3,2,1,0:T(8,128)(2,1)S(1)}, bf16[4,1,64,258]{3,2,1,0:T(8,128)(2,1)S(1)}, u32[]{:S(2)}, u32[]{:S(2)}) collective-permute-start(bf16[4,1,64,258]{3,2,1,0:T(8,128)(2,1)S(1)} %get-tuple-element.160), channel_id=1, source_target_pairs={{0,1},{1,2},{2,3},{3,4},{4,5},{5,6},{6,7},{8,9},{9,10},{10,11},{11... | collective-permute-start | bytes 396296 | tf_op jit(solution)/shard_map/ppermute | solution.py:22
  83.2 1.1 copy-start.3
  83.2 1.3 copy-start.5
  129.9 1.3 copy-start.8
  129.9 2.3 copy-start.10
  131.2 2.0 copy-start.6
  131.2 3.0 copy-start.4
  134.2 2.9 copy-start.2
  137.1 10.3 %copy-start.11 = (bf16[4,4,64,256]{3,2,1,0:T(8,128)(2,1)S(1)}, bf16[4,4,64,256]{3,2,1,0:T(8,128)(2,1)}, u32[]{:S(2)}) copy-start(bf16[4,4,64,256]{3,2,1,0:T(8,128)(2,1)} %get-tuple-element.167) | copy-start | bytes 1572868
  140.4 127.0 %collective-permute-start.6 = (bf16[4,64,258]{2,1,0:T(8,128)(2,1)}, bf16[4,64,258]{2,1,0:T(8,128)(2,1)}, u32[]{:S(2)}, u32[]{:S(2)}) collective-permute-start(bf16[4,64,258]{2,1,0:T(8,128)(2,1)} %get-tuple-element.156), channel_id=1, source_target_pairs={{0,1},{1,2},{2,3},{3,4},{4,5},{5,6},{6,7},{8,9},{9,10},{10,11},{11... | collective-permute-start | bytes 396296 | tf_op jit(solution)/shard_map/ppermute | solution.py:31
  144.8 125.8 %collective-permute-start.7 = (bf16[4,64,258]{2,1,0:T(8,128)(2,1)}, bf16[4,64,258]{2,1,0:T(8,128)(2,1)}, u32[]{:S(2)}, u32[]{:S(2)}) collective-permute-start(bf16[4,64,258]{2,1,0:T(8,128)(2,1)} %get-tuple-element.155), channel_id=1, source_target_pairs={{1,0},{2,1},{3,2},{4,3},{5,4},{6,5},{7,6},{9,8},{10,9},{11,10},{12... | collective-permute-start | bytes 396296 | tf_op jit(solution)/shard_map/ppermute | solution.py:31
  273.0 4.3 %collective-permute-start.8 = (bf16[4,32,64]{2,0,1:T(4,128)(2,1)S(1)}, bf16[4,32,64]{2,0,1:T(4,128)(2,1)S(1)}, u32[]{:S(2)}, u32[]{:S(2)}) collective-permute-start(bf16[4,32,64]{2,0,1:T(4,128)(2,1)S(1)} %convert_element_type.38), channel_id=1, source_target_pairs={{8,0},{0,8},{9,1},{1,9},{10,2},{2,10},{11,3},{3,11},{12,4},{4,12},... | collective-permute-start | bytes 49160 | tf_op jit(solution)/shard_map/ppermute | solution.py:12
  275.2 4.0 %collective-permute-start.9 = (bf16[4,32,64]{2,0,1:T(4,128)(2,1)S(1)}, bf16[4,32,64]{2,0,1:T(4,128)(2,1)S(1)}, u32[]{:S(2)}, u32[]{:S(2)}) collective-permute-start(bf16[4,32,64]{2,0,1:T(4,128)(2,1)S(1)} %convert_element_type.39), channel_id=1, source_target_pairs={{8,0},{0,8},{9,1},{1,9},{10,2},{2,10},{11,3},{3,11},{12,4},{4,12},... | collective-permute-start | bytes 49160 | tf_op jit(solution)/shard_map/ppermute | solution.py:12
Sparse Core Ops, SparseCore 0:
  137.3 128.2 all-reduce.5
where the time goes:
time: 318 us; the launch traced here: 317 us
  blocking collectives  120 us (38%)
  waiting for transfers between devices  74.3 us (23%)
  local copies, waits for them, and re-layouts  49.8 us (16%)
  matrix products  27.6 us (9%)
  starting transfers between devices  20.2 us (6%)
  between operations  15.2 us (5%)
  other arithmetic  9.59 us (3%)
    psum x1, waiting for transfers between devices, shards(): lax.psum((hex_local, time_local), ('tm', 'diamond', 'tile'))  71.3 us
    psum x1, blocking collectives, shards(): lax.psum((hex_local, time_local), ('tm', 'diamond', 'tile'))  45.7 us
    scatter-add x5, local copies, waits for them, and re-layouts, shards(): spread = spread.at[:, 1 + step_row:1 + step_row + tile_rows, :, 1 + step_...  30.8 us
    unnamed x1, blocking collectives  26.9 us
    all_gather x1, blocking collectives, shards(): lax.all_gather(field[..., 0], 'tile', axis=1, tiled=True)  25.1 us
    all_gather x1, blocking collectives, shards(): lax.all_gather(field[..., columns - 1], 'tile', axis=1, tiled=True)  22.7 us
    dot_general x7, matrix products, shards(): jnp.einsum('frdx,cd->frcx', grad_wide, hex_weight[number], preferred_elem...  9.43 us
    ppermute x2, starting transfers between devices, with_halo(): before = lax.ppermute(last, axis, up)  7.4 us
  transfers between devices with their start and end apart: 11, of which 3 were waited for; matrix products, arithmetic and copies ran while one was open for 9% of the time, Pallas kernels for 0%

commit v1 on v0

--- a/solution.py
+++ b/solution.py
@@ -4,6 +4,34 @@
 from jax.sharding import PartitionSpec as P
 
 OFFSETS = ((0, 0), (0, 1), (0, -1), (1, 0), (-1, 0), (1, -1), (-1, 1))
+
+
+def deliver_local_data_up(x_in, array_dim):
+    x_in = jnp.moveaxis(x_in, 0, array_dim)
+    kept_arr = x_in.shape
+    b_now = x_in.reshape(
+        *kept_arr[:array_dim],
+        kept_arr[array_dim] * kept_arr[array_dim + 1],
+        *kept_arr[array_dim + 2 :]
+    )
+    return b_now
+
+
+def fit_routes_all_by_axis(panel, axis_key):
+    count_all = lax.axis_size(axis_key)
+    e_next = panel[None]
+    for idx in range(count_all.bit_length() - 1):
+        wide_out = 1 << idx
+        plain = lax.ppermute(e_next, axis_key, tuple(((p, p ^ wide_out) for p in range(count_all))))
+        s_next = jnp.stack([e_next, plain])
+        view_out = lax.axis_index(axis_key) >> idx & 1
+        e_next = jnp.where(view_out == 0, s_next, s_next[::-1]).reshape(-1, *panel.shape)
+    return e_next
+
+
+def attach_the_ticks(dim_no, local, u="tile"):
+    x_next = deliver_local_data_up(fit_routes_all_by_axis(local, u), dim_no)
+    return x_next
 
 
 def from_behind(block, axis, distance):
@@ -46,7 +74,7 @@
     own_left = lax.dynamic_slice(left_map, (chart, first_row), (1, tile_rows))[0]
     own_right = lax.dynamic_slice(right_map, (chart, first_row), (1, tile_rows))[0]
     strips = (
-        lax.all_gather(field[..., 0], "tile", axis=1, tiled=True),
+        attach_the_ticks(1, local=field[..., 0]),
         lax.all_gather(field[..., columns - 1], "tile", axis=1, tiled=True),
     )
     prev_right = from_behind(strips[1], "diamond", 1)

time: 318 us -> 306 us (0.962)
  blocking collectives: 120 us -> 96.8 us
  waiting for transfers between devices: 74.3 us -> 80.8 us
  starting transfers between devices: 20.2 us -> 23.5 us
    all_gather x1 -> x0, blocking collectives: 25.1 us -> none  [shards(): lax.all_gather(field[..., 0], 'tile', axis=1, tiled=True)]
    ppermute x0 -> x3, waiting for transfers between devices: none -> 4 us  [fit_routes_all_by_axis(): lax.ppermute(e_next, axis_key, tuple(((p, p ^ wide_out) for p in range(co...]
    ppermute x0 -> x3, starting transfers between devices: none -> 3.58 us  [fit_routes_all_by_axis(): lax.ppermute(e_next, axis_key, tuple(((p, p ^ wide_out) for p in range(co...]
  transfers between devices with their start and end apart: 11 -> 14, of which waited for: 3 -> 6; matrix products, arithmetic and copies ran while one was open for 9% -> 10% of each run, Pallas kernels for 0% -> 0%
where the time goes in v1:
time: 306 us; the launch traced here: 305 us
  blocking collectives  96.8 us (32%)
  waiting for transfers between devices  80.8 us (26%)
  local copies, waits for them, and re-layouts  49.7 us (16%)
  matrix products  29.6 us (10%)
  starting transfers between devices  23.5 us (8%)
  between operations  15.2 us (5%)
  other arithmetic  9.74 us (3%)
    psum x1, waiting for transfers between devices, shards(): lax.psum((hex_local, time_local), ('tm', 'diamond', 'tile'))  71.6 us
    psum x1, blocking collectives, shards(): lax.psum((hex_local, time_local), ('tm', 'diamond', 'tile'))  45.1 us
    scatter-add x5, local copies, waits for them, and re-layouts, shards(): spread = spread.at[:, 1 + step_row:1 + step_row + tile_rows, :, 1 + step_...  30.9 us
    unnamed x1, blocking collectives  26.9 us
    all_gather x1, blocking collectives, shards(): lax.all_gather(field[..., columns - 1], 'tile', axis=1, tiled=True)  24.8 us
    dot_general x7, matrix products, shards(): jnp.einsum('frdx,cd->frcx', grad_wide, hex_weight[number], preferred_elem...  9.58 us
    ppermute x2, starting transfers between devices, with_halo(): before = lax.ppermute(last, axis, up)  7.42 us
    dot_general x7, matrix products, shards(): jnp.einsum('frcx,frdx->cd', window, grad_wide, preferred_element_type=jnp...  6.82 us
  transfers between devices with their start and end apart: 14, of which 6 were waited for; matrix products, arithmetic and copies ran while one was open for 10% of the time, Pallas kernels for 0%

profile of v1, /device:TPU:0, one launch (start us, length us, event | category | flops | bytes accessed | tf_op | source)
XLA Modules:
  0.0 305.3 jit_solution(10522649605461534815)
XLA Ops:
  9.1 24.8 %all-gather = bf16[4,32,64,1]{3,2,1,0:T(8,128)(2,1)S(1)} all-gather(bf16[4,4,64,1]{3,2,1,0:T(8,128)(2,1)S(1)} %get-tuple-element.163), channel_id=2, replica_groups=mesh['tm'=2,'diamond'=2,'tile'=8] {'tile'}, dimensions={1}, use_global_device_ids=true | all-gather | bytes 18432 | tf_op jit(solution)/shard_map/all_gather | solution.py:78
  34.9 1.6 collective-permute-start.6
  37.2 4.1 %collective-permute-start.1 = (bf16[1,4,64,256]{3,2,1,0:T(8,128)(2,1)}, bf16[1,4,64,256]{3,2,1,0:T(8,128)(2,1)}, u32[]{:S(2)}, u32[]{:S(2)}) collective-permute-start(bf16[1,4,64,256]{3,2,1,0:T(8,128)(2,1)} %get-tuple-element.162), channel_id=1, source_target_pairs={{0,16},{1,17},{2,18},{3,19},{4,20},{5,21},{6,22},{7,23},{8,24},{9,... | collective-permute-start | bytes 393224 | tf_op jit(solution)/shard_map/ppermute | solution.py:50
  42.7 2.0 convolution_bitcast_fusion.16
  45.9 2.7 and_reduce_fusion
  49.9 2.5 collective-permute-done.3
  52.5 1.9 collective-permute-start.4
  55.7 1.5 collective-permute-done.4
  59.2 2.1 collective-permute-done.5
  63.1 1.4 convolution_bitcast_fusion.12
  64.6 1.4 collective-permute-start.7
  66.0 3.4 %collective-permute-start.8 = (bf16[4,1,64,258]{3,2,1,0:T(8,128)(2,1)S(1)}, bf16[4,1,64,258]{3,2,1,0:T(8,128)(2,1)S(1)}, u32[]{:S(2)}, u32[]{:S(2)}) collective-permute-start(bf16[4,1,64,258]{3,2,1,0:T(8,128)(2,1)S(1)} %get-tuple-element.160), channel_id=1, source_target_pairs={{0,1},{1,2},{2,3},{3,4},{4,5},{5,6},{6,7},{8,9},{9,10},{10,11},{11... | collective-permute-start | bytes 396296 | tf_op jit(solution)/shard_map/ppermute | solution.py:50
  73.0 1.5 multiply_convert_fusion
  74.5 1.5 fusion.15
  77.1 1.4 fusion.9
  79.0 7.1 %scatter-add.39 = f32[4,6,64,258]{3,2,0,1:T(8,128)S(1)} dynamic-update-slice(f32[4,6,64,258]{3,2,0,1:T(8,128)S(1)} %scatter-add.36, f32[4,4,64,256]{3,2,0,1:T(8,128)} %fusion.9, s32[]{:T(128)} %constant.334.clone.1, s32[]{:T(128)} %constant.333.clone.1, s32[]{:T(128)} %constant.334.clone.1, s32[]{:T(128)} %constant.332.clone.1) | dynamic-update-slice | bytes 2097156 | tf_op jit(solution)/shard_map/scatter-add | solution.py:121
  87.8 7.1 %scatter-add.41 = f32[4,6,64,258]{3,2,0,1:T(8,128)S(1)} dynamic-update-slice(f32[4,6,64,258]{3,2,0,1:T(8,128)S(1)} %fusion.11, f32[4,4,64,256]{3,2,0,1:T(8,128)} %fusion.12, s32[]{:T(128)} %constant.334.clone.1, s32[]{:T(128)} %constant.332.clone.1, s32[]{:T(128)} %constant.334.clone.1, s32[]{:T(128)} %constant.333.clone.1) | dynamic-update-slice | bytes 2097156 | tf_op jit(solution)/shard_map/scatter-add | solution.py:121
  94.8 2.7 add_select_fusion.1
  97.5 7.8 %scatter-add.44 = f32[4,6,64,258]{3,2,0,1:T(8,128)S(1)} dynamic-update-slice(f32[4,6,64,258]{3,2,0,1:T(8,128)S(1)} %scatter-add.41, f32[4,4,64,256]{3,2,0,1:T(8,128)} %add_select_fusion.1, s32[]{:T(128)} %constant.334.clone.1, s32[]{:T(128)S(1)} %bitcast.387, s32[]{:T(128)} %constant.334.clone.1, s32[]{:T(128)} %bitcast.70) | dynamic-update-slice | bytes 2097156 | tf_op jit(solution)/shard_map/scatter-add | solution.py:121
  105.6 3.3 %add_select_fusion = f32[4,4,64,256]{3,2,0,1:T(8,128)} fusion(f32[4,6,64,258]{3,2,0,1:T(8,128)S(1)} %fusion.14, s32[]{:T(128)} %bitcast.75, s32[]{:T(128)} %bitcast.76, pred[]{:T(512)} %get-tuple-element.147, bf16[4,4,64,256]{3,2,1,0:T(8,128)(2,1)S(1)} %fusion.15, bf16[7,64,64]{2,1,0:T(8,128)(2,1)S(1)} %copy-done.14), kind=kOutput, calls=%fused_computation.4 | convolution fusion | flops 34078720 | bytes 2637833 | tf_op jit(solution)/shard_map/frdx,cd->frcx/dot_general | solution.py:122
  108.9 8.4 %scatter-add.46 = f32[4,6,64,258]{3,2,0,1:T(8,128)S(1)} dynamic-update-slice(f32[4,6,64,258]{3,2,0,1:T(8,128)S(1)} %fusion.14, f32[4,4,64,256]{3,2,0,1:T(8,128)} %add_select_fusion, s32[]{:T(128)} %constant.334.clone.1, s32[]{:T(128)} %bitcast.75, s32[]{:T(128)} %constant.334.clone.1, s32[]{:T(128)} %bitcast.76) | dynamic-update-slice | bytes 2097156 | tf_op jit(solution)/shard_map/scatter-add | solution.py:121
  125.8 1.9 slice_bitcast_fusion.1
  127.7 4.1 %collective-permute-start.9 = (bf16[4,64,258]{2,1,0:T(8,128)(2,1)}, bf16[4,64,258]{2,1,0:T(8,128)(2,1)}, u32[]{:S(2)}, u32[]{:S(2)}) collective-permute-start(bf16[4,64,258]{2,1,0:T(8,128)(2,1)} %get-tuple-element.156), channel_id=1, source_target_pairs={{0,1},{1,2},{2,3},{3,4},{4,5},{5,6},{6,7},{8,9},{9,10},{10,11},{11... | collective-permute-start | bytes 396296 | tf_op jit(solution)/shard_map/ppermute | solution.py:59
  137.0 45.1 %psum.15 = f32[3,64,64]{2,1,0:T(8,128)} all-reduce(f32[3,64,64]{2,1,0:T(8,128)S(1)} %pad_maximum_fusion.16), channel_id=1, replica_groups=mesh['tm'=2,'diamond'=2,'tile'=8] {'tm','diamond','tile'}, use_global_device_ids=true, to_apply=%region_7.9 | all-reduce | flops 12288 | bytes 98304 | tf_op jit(solution)/shard_map/psum | solution.py:160
  182.1 71.6 %all-reduce.6.cloned.1.call-done = f32[7,64,64]{1,2,0:T(8,128)} async-done(((f32[7,64,64]{1,2,0:T(8,128)}), f32[7,64,64]{1,2,0:T(8,128)}) %all-reduce.6.cloned.1.call-update) | async-done | bytes 114704 | tf_op jit(solution)/shard_map/psum | solution.py:160
  253.7 1.8 copy.135
  255.5 1.7 fusion.33
  257.2 1.5 copy.121
  261.1 1.5 collective-permute-start.11
  265.3 1.9 collective-permute-done.12
  267.3 26.9 %all-reduce.3 = (bf16[4,32,64]{2,0,1:T(4,128)(2,1)S(1)}, bf16[4,32,64]{2,0,1:T(4,128)(2,1)S(1)}) all-reduce(bf16[4,32,64]{2,0,1:T(4,128)(2,1)S(1)} %collective-permute-done.11, bf16[4,32,64]{2,0,1:T(4,128)(2,1)S(1)} %collective-permute-done.12), channel_id=3, replica_groups=mesh['tm'=2,'diamond'=2,'tile'=8] {'tile'}, use_global_device_ids=true, to_apply=%region_3.5.clone | all-reduce | flops 16384 | bytes 65536
  295.0 1.9 scatter-add.51
  (132 shorter events, 40.1 us)
Async XLA Ops:
  7.2 246.6 %all-reduce.6.cloned.1.call-start = ((), (), s32[]{:S(2)}) async-start(), calls=%async_computation | async-start | bytes 458752 | tf_op jit(solution)/shard_map/psum | solution.py:160
  8.5 40.1 %collective-permute-start.2 = (bf16[1,4,4,64]{3,2,1,0:T(4,128)(2,1)S(1)}, bf16[1,4,4,64]{3,2,1,0:T(4,128)(2,1)S(1)}, u32[]{:S(2)}, u32[]{:S(2)}) collective-permute-start(bf16[1,4,4,64]{3,2,1,0:T(4,128)(2,1)S(1)} %bitcast.381), channel_id=1, source_target_pairs={{0,1},{1,0},{2,3},{3,2},{4,5},{5,4},{6,7},{7,6},{8,9},{9,8},{10,11... | collective-permute-start | bytes 6152 | tf_op jit(solution)/shard_map/ppermute | solution.py:25
  9.1 27.4 %copy-start.1 = (bf16[4,1,4,64,256]{4,3,2,1,0:T(8,128)(2,1)S(1)}, bf16[4,1,4,64,256]{4,3,2,1,0:T(8,128)(2,1)}, u32[]{:S(2)}) copy-start(bf16[4,1,4,64,256]{4,3,2,1,0:T(8,128)(2,1)} %param.31) | copy-start | bytes 1572868
  9.1 33.5 %copy-start.16 = (s32[2,32]{1,0:T(2,128)S(1)}, s32[2,32]{1,0:T(2,128)}, u32[]{:S(2)}) copy-start(s32[2,32]{1,0:T(2,128)} %param.35) | copy-start | bytes 772
  33.8 12.1 %copy-start.18 = (s32[4]{0:T(128)S(1)}, s32[4]{0:T(128)}, u32[]{:S(2)}) copy-start(s32[4]{0:T(128)} %constant.341.clone.1) | copy-start | bytes 52
  33.8 14.8 %copy-start.17 = (s32[2,32]{1,0:T(2,128)S(1)}, s32[2,32]{1,0:T(2,128)}, u32[]{:S(2)}) copy-start(s32[2,32]{1,0:T(2,128)} %param.34) | copy-start | bytes 772
  33.8 20.6 %copy-start.19 = (u32[32]{0:T(128)S(1)}, u32[32]{0:T(128)}, u32[]{:S(2)}) copy-start(u32[32]{0:T(128)} %constant.351) | copy-start | bytes 388
  34.9 23.9 %copy-start = (bf16[4,1,4,64,256]{4,3,2,1,0:T(8,128)(2,1)S(1)}, bf16[4,1,4,64,256]{4,3,2,1,0:T(8,128)(2,1)}, u32[]{:S(2)}) copy-start(bf16[4,1,4,64,256]{4,3,2,1,0:T(8,128)(2,1)} %param.30) | copy-start | bytes 1572868
  34.9 23.9 %copy-start.14 = (bf16[7,64,64]{2,1,0:T(8,128)(2,1)S(1)}, bf16[7,64,64]{2,1,0:T(8,128)(2,1)}, u32[]{:S(2)}) copy-start(bf16[7,64,64]{2,1,0:T(8,128)(2,1)} %param.32) | copy-start | bytes 172036
  34.9 23.0 %collective-permute-start.6 = (bf16[4,32,64]{2,0,1:T(4,128)(2,1)S(1)}, bf16[4,32,64]{2,0,1:T(4,128)(2,1)S(1)}, u32[]{:S(2)}, u32[]{:S(2)}) collective-permute-start(bf16[4,32,64]{2,0,1:T(4,128)(2,1)S(1)} %bitcast.376), channel_id=1, source_target_pairs={{8,0},{0,8},{9,1},{1,9},{10,2},{2,10},{11,3},{3,11},{12,4},{4,12},... | collective-permute-start | bytes 49160 | tf_op jit(solution)/shard_map/ppermute | solution.py:40
  37.2 32.5 %collective-permute-start.1 = (bf16[1,4,64,256]{3,2,1,0:T(8,128)(2,1)}, bf16[1,4,64,256]{3,2,1,0:T(8,128)(2,1)}, u32[]{:S(2)}, u32[]{:S(2)}) collective-permute-start(bf16[1,4,64,256]{3,2,1,0:T(8,128)(2,1)} %get-tuple-element.162), channel_id=1, source_target_pairs={{0,16},{1,17},{2,18},{3,19},{4,20},{5,21},{6,22},{7,23},{8,24},{9,... | collective-permute-start | bytes 393224 | tf_op jit(solution)/shard_map/ppermute | solution.py:50
  41.3 33.2 %collective-permute-start = (bf16[1,4,64,256]{3,2,1,0:T(8,128)(2,1)}, bf16[1,4,64,256]{3,2,1,0:T(8,128)(2,1)}, u32[]{:S(2)}, u32[]{:S(2)}) collective-permute-start(bf16[1,4,64,256]{3,2,1,0:T(8,128)(2,1)} %get-tuple-element.161), channel_id=1, source_target_pairs={{16,0},{17,1},{18,2},{19,3},{20,4},{21,5},{22,6},{23,7},{24,8},{25... | collective-permute-start | bytes 393224 | tf_op jit(solution)/shard_map/ppermute | solution.py:51
  48.7 3.7 %collective-permute-start.3 = (bf16[2,4,4,64]{3,2,1,0:T(4,128)(2,1)S(1)}, bf16[2,4,4,64]{3,2,1,0:T(4,128)(2,1)S(1)}, u32[]{:S(2)}, u32[]{:S(2)}) collective-permute-start(bf16[2,4,4,64]{3,2,1,0:T(4,128)(2,1)S(1)} %get-tuple-element.166), channel_id=1, source_target_pairs={{0,2},{1,3},{2,0},{3,1},{4,6},{5,7},{6,4},{7,5},{8,10},{9,11},{10,... | collective-permute-start | bytes 12296 | tf_op jit(solution)/shard_map/ppermute | solution.py:25
  52.5 4.7 %collective-permute-start.4 = (bf16[4,4,4,64]{3,2,1,0:T(4,128)(2,1)S(1)}, bf16[4,4,4,64]{3,2,1,0:T(4,128)(2,1)S(1)}, u32[]{:S(2)}, u32[]{:S(2)}) collective-permute-start(bf16[4,4,4,64]{3,2,1,0:T(4,128)(2,1)S(1)} %bitcast.374), channel_id=1, source_target_pairs={{0,4},{1,5},{2,6},{3,7},{4,0},{5,1},{6,2},{7,3},{8,12},{9,13},{10,... | collective-permute-start | bytes 24584 | tf_op jit(solution)/shard_map/ppermute | solution.py:25
  57.3 4.0 %collective-permute-start.5 = (bf16[4,32,64]{2,0,1:T(4,128)(2,1)S(1)}, bf16[4,32,64]{2,0,1:T(4,128)(2,1)S(1)}, u32[]{:S(2)}, u32[]{:S(2)}) collective-permute-start(bf16[4,32,64]{2,0,1:T(4,128)(2,1)S(1)} %copy.92), channel_id=1, source_target_pairs={{8,0},{0,8},{9,1},{1,9},{10,2},{2,10},{11,3},{3,11},{12,4},{4,12},... | collective-permute-start | bytes 49160 | tf_op jit(solution)/shard_map/ppermute | solution.py:40
  58.8 12.2 %copy-start.7 = (bf16[4,4,64,1]{3,2,1,0:T(8,128)(2,1)}, bf16[4,4,64,1]{3,2,1,0:T(8,128)(2,1)S(1)}, u32[]{:S(2)}) copy-start(bf16[4,4,64,1]{3,2,1,0:T(8,128)(2,1)S(1)} %copy.98) | copy-start | bytes 6148
  64.6 5.2 %copy-start.15 = (bf16[3,64,64]{2,1,0:T(8,128)(2,1)S(1)}, bf16[3,64,64]{2,1,0:T(8,128)(2,1)}, u32[]{:S(2)}) copy-start(bf16[3,64,64]{2,1,0:T(8,128)(2,1)} %param.33) | copy-start | bytes 73732
  64.6 6.3 %collective-permute-start.7 = (bf16[4,1,64,258]{3,2,1,0:T(8,128)(2,1)S(1)}, bf16[4,1,64,258]{3,2,1,0:T(8,128)(2,1)S(1)}, u32[]{:S(2)}, u32[]{:S(2)}) collective-permute-start(bf16[4,1,64,258]{3,2,1,0:T(8,128)(2,1)S(1)} %get-tuple-element.159), channel_id=1, source_target_pairs={{1,0},{2,1},{3,2},{4,3},{5,4},{6,5},{7,6},{9,8},{10,9},{11,10},{12... | collective-permute-start | bytes 396296 | tf_op jit(solution)/shard_map/ppermute | solution.py:51
  66.0 4.9 %copy-start.10 = (bf16[4,4,64,1]{3,2,1,0:T(8,128)(2,1)S(1)}, bf16[4,4,64,1]{3,2,1,0:T(8,128)(2,1)}, u32[]{:S(2)}) copy-start(bf16[4,4,64,1]{3,2,1,0:T(8,128)(2,1)} %copy-done.9) | copy-start | bytes 6148
  66.0 4.9 %collective-permute-start.8 = (bf16[4,1,64,258]{3,2,1,0:T(8,128)(2,1)S(1)}, bf16[4,1,64,258]{3,2,1,0:T(8,128)(2,1)S(1)}, u32[]{:S(2)}, u32[]{:S(2)}) collective-permute-start(bf16[4,1,64,258]{3,2,1,0:T(8,128)(2,1)S(1)} %get-tuple-element.160), channel_id=1, source_target_pairs={{0,1},{1,2},{2,3},{3,4},{4,5},{5,6},{6,7},{8,9},{9,10},{10,11},{11... | collective-permute-start | bytes 396296 | tf_op jit(solution)/shard_map/ppermute | solution.py:50
  71.7 1.3 copy-start.5
  73.0 1.5 copy-start.13
  118.6 1.3 copy-start.11
  118.6 2.3 copy-start.8
  119.8 2.0 copy-start.6
  119.8 3.0 copy-start.4
  122.9 10.2 %copy-start.2 = (bf16[4,1,4,64,256]{4,3,2,1,0:T(8,128)(2,1)S(1)}, bf16[4,1,4,64,256]{4,3,2,1,0:T(8,128)(2,1)}, u32[]{:S(2)}) copy-start(bf16[4,1,4,64,256]{4,3,2,1,0:T(8,128)(2,1)} %param.31) | copy-start | bytes 1572868
  125.8 10.0 %copy-start.12 = (bf16[4,4,64,256]{3,2,1,0:T(8,128)(2,1)S(1)}, bf16[4,4,64,256]{3,2,1,0:T(8,128)(2,1)}, u32[]{:S(2)}) copy-start(bf16[4,4,64,256]{3,2,1,0:T(8,128)(2,1)} %get-tuple-element.169) | copy-start | bytes 1572868
  127.7 127.8 %collective-permute-start.9 = (bf16[4,64,258]{2,1,0:T(8,128)(2,1)}, bf16[4,64,258]{2,1,0:T(8,128)(2,1)}, u32[]{:S(2)}, u32[]{:S(2)}) collective-permute-start(bf16[4,64,258]{2,1,0:T(8,128)(2,1)} %get-tuple-element.156), channel_id=1, source_target_pairs={{0,1},{1,2},{2,3},{3,4},{4,5},{5,6},{6,7},{8,9},{9,10},{10,11},{11... | collective-permute-start | bytes 396296 | tf_op jit(solution)/shard_map/ppermute | solution.py:59
  131.8 126.9 %collective-permute-start.10 = (bf16[4,64,258]{2,1,0:T(8,128)(2,1)}, bf16[4,64,258]{2,1,0:T(8,128)(2,1)}, u32[]{:S(2)}, u32[]{:S(2)}) collective-permute-start(bf16[4,64,258]{2,1,0:T(8,128)(2,1)} %get-tuple-element.155), channel_id=1, source_target_pairs={{1,0},{2,1},{3,2},{4,3},{5,4},{6,5},{7,6},{9,8},{10,9},{11,10},{12... | collective-permute-start | bytes 396296 | tf_op jit(solution)/shard_map/ppermute | solution.py:59
  261.1 4.3 %collective-permute-start.11 = (bf16[4,32,64]{2,0,1:T(4,128)(2,1)S(1)}, bf16[4,32,64]{2,0,1:T(4,128)(2,1)S(1)}, u32[]{:S(2)}, u32[]{:S(2)}) collective-permute-start(bf16[4,32,64]{2,0,1:T(4,128)(2,1)S(1)} %convert_element_type.38), channel_id=1, source_target_pairs={{8,0},{0,8},{9,1},{1,9},{10,2},{2,10},{11,3},{3,11},{12,4},{4,12},... | collective-permute-start | bytes 49160 | tf_op jit(solution)/shard_map/ppermute | solution.py:40
  263.3 4.0 %collective-permute-start.12 = (bf16[4,32,64]{2,0,1:T(4,128)(2,1)S(1)}, bf16[4,32,64]{2,0,1:T(4,128)(2,1)S(1)}, u32[]{:S(2)}, u32[]{:S(2)}) collective-permute-start(bf16[4,32,64]{2,0,1:T(4,128)(2,1)S(1)} %convert_element_type.39), channel_id=1, source_target_pairs={{8,0},{0,8},{9,1},{1,9},{10,2},{2,10},{11,3},{3,11},{12,4},{4,12},... | collective-permute-start | bytes 49160 | tf_op jit(solution)/shard_map/ppermute | solution.py:40
  (2 other events, 1.8 us)
Sparse Core Ops, SparseCore 0:
  125.9 127.7 all-reduce.5
